TPU v7x, 512 devices: a whole 4x4x16 slice. The times are simulated.
512 devices in a mesh: leaf: 32 (over z, core), front: 16 (over y, x).
Axes of the slice: x: 4, y: 4, z: 16, core: 2. Of those that a mesh axis runs over, the one named last changes fastest.
Arguments:
- parent_border_inverse: float32 [32, 1536, 1536], P('leaf', 'front')
- parent_border_rows: float32 [32, 1536, 768], P('leaf', 'front'), may hold values from -0.09 to 0.09
- parent_diagonal_inverse: float32 [32, 768, 768], P('leaf', 'front')
- child_border_rows: float32 [64, 1024, 512], P('leaf', 'front'), may hold values from -0.13 to 0.13
- child_factor_inverse: float32 [64, 512, 512], P('leaf', 'front')
- child_index: int32 [64, 1024], replicated, may hold values from 0 to 2303, as said below
- child_parent: int32 [64], replicated, may hold values from 0 to 31, as said below
Outputs:
- parent_variance: float32 [32, 768], P('leaf')
- child_variance: float32 [64, 512], P('leaf')
Inputs may be any that keep to these rules, and one draw needn't show every extreme that they name: `child_index`: each row holds 1024 distinct positions in increasing order, the first 0 and the last 2303. `child_parent`: child c's parent is c // 2 or c // 2 with its lowest bit flipped, and every parent has exactly two children.
All inputs are finite; a program needn't handle non-finite values.
Results may differ from a plain program's by a relative error of at most 0.0003.
Values sent between devices are 32-bit elements; how exact they have to be, the bound alone decides.
A program may use at most 64 MiB of HBM per device.

v0:
```python
import jax
import jax.numpy as jnp
from jax import lax
from jax.sharding import PartitionSpec as P

ELIMINATED_SIZE = 768
BORDER_SIZE = 1536
CHILD_ELIMINATED = 512


def partner_2(value, axis, distance):
    mask = 2**distance
    pairs = [(source, source ^ mask) for source in range(lax.axis_size(axis))]
    return lax.ppermute(value, axis, pairs)


def matrix_product(left, right):
    return jnp.dot(left, right, precision=lax.Precision.HIGHEST, preferred_element_type=jnp.float32)


def batched_fronts(form, left, right):
    return jnp.einsum(
        form, left, right, precision=lax.Precision.HIGHEST, preferred_element_type=jnp.float32
    )


def folded_rows(left_matrix, block_rows):
    return matrix_product(left_matrix, block_rows)


def children_of(child_parent, owner):
    partner = jnp.bitwise_xor(owner, 1)
    pool_ids = jnp.stack([2 * owner, 2 * owner + 1, 2 * partner, 2 * partner + 1])
    member = (jnp.take(child_parent, pool_ids) == owner).astype(jnp.int32)
    first = jnp.argmax(member)
    second = 3 - jnp.argmax(member[::-1])
    slots = jnp.stack([first, second])
    return (slots, jnp.take(pool_ids, slots))


def shards(
    parent_border_inverse,
    parent_border_rows,
    parent_diagonal_inverse,
    child_border_rows,
    child_factor_inverse,
    child_index,
    child_parent,
):
    border_inverse = parent_border_inverse[0]
    border_factor = parent_border_rows[0]
    eliminated_inverse = parent_diagonal_inverse[0]
    border_rows = border_inverse.shape[0]
    weight_rows = folded_rows(
        border_factor, lax.all_gather(eliminated_inverse, "front", axis=0, tiled=True)
    )
    own_weights = batched_fronts(
        "krj,kjm->krm",
        child_border_rows,
        lax.all_gather(child_factor_inverse, "front", axis=1, tiled=True),
    )
    leaf_index = lax.axis_index("leaf")
    partner = jnp.bitwise_xor(leaf_index, 1)
    partner_weights = partner_2(own_weights, "leaf", 0)
    pooled = jnp.concatenate([own_weights, partner_weights], axis=0)
    slots, kid_ids = children_of(child_parent, leaf_index)
    selected = jnp.take(pooled, slots, axis=0)
    child_weight = lax.all_gather(selected, "front", axis=1, tiled=True)
    index_list = jnp.take(child_index, kid_ids, axis=0)
    placed_rows = (
        jnp.zeros((2, ELIMINATED_SIZE + BORDER_SIZE, CHILD_ELIMINATED), jnp.float32)
        .at[jnp.arange(2)[:, None], index_list]
        .set(child_weight)
    )
    upper_block = placed_rows[:, :ELIMINATED_SIZE]
    lower_block = placed_rows[:, ELIMINATED_SIZE:]
    own_lower = lax.dynamic_slice_in_dim(
        lower_block, lax.axis_index("front") * border_rows, border_rows, 1
    )
    reduced = own_lower - batched_fronts("zt,qtg->qzg", weight_rows, upper_block)
    border_product = folded_rows(
        border_inverse, lax.all_gather(weight_rows, "front", axis=0, tiled=True)
    )
    parent_block = jnp.sum(eliminated_inverse * eliminated_inverse, axis=0) + jnp.sum(
        weight_rows * border_product, axis=0
    )
    kid_image = batched_fronts("rb,kbm->krm", border_inverse, lower_block) - batched_fronts(
        "zt,qtg->qzg", border_product, upper_block
    )
    lifted_rows = batched_fronts("zt,qtg->qzg", eliminated_inverse, upper_block)
    quad_part = jnp.sum(lifted_rows * lifted_rows, axis=1) + jnp.sum(reduced * kid_image, axis=1)
    own_part = jnp.sum(child_factor_inverse * child_factor_inverse, axis=1)
    parent_total, quad_total, own_total = lax.psum((parent_block, quad_part, own_part), "front")
    returned = partner_2(quad_total, "leaf", 0)
    partner_slots, partner_ids = children_of(child_parent, partner)
    mine = 2 * leaf_index + jnp.arange(2, dtype=jnp.int32)
    from_self = (kid_ids[None, :] == mine[:, None]).astype(jnp.float32)
    from_partner = (partner_ids[None, :] == mine[:, None]).astype(jnp.float32)
    kid_quadratic = matrix_product(from_self, quad_total) + matrix_product(from_partner, returned)
    return (parent_total[None], own_total + kid_quadratic)


def solution(mesh):
    in_specs = (
        P("leaf", "front", None),
        P("leaf", "front", None),
        P("leaf", "front", None),
        P("leaf", "front", None),
        P("leaf", "front", None),
        P(),
        P(),
    )
    out_specs = (P("leaf", None), P("leaf", None))
    return jax.shard_map(shards, mesh=mesh, in_specs=in_specs, out_specs=out_specs, check_vma=False)
```

profile of v0, /device:TPU:1, one launch (start us, length us, event | category | flops | bytes accessed | tf_op | source)
XLA Modules:
  0.0 379.8 jit_solution(9751702435656411364)
XLA Ops:
  7.2 0.0 copy-start
  7.2 0.0 copy-start.6
  7.2 0.0 all-gather.8.cloned.1.call-start
  7.2 0.7 all-gather.8.cloned.1.call-update
  7.9 0.0 all-gather.12.cloned.1.call-start
  8.0 0.7 all-gather.12.cloned.1.call-update
  8.7 0.0 all-gather.10.cloned.1.call-start
  8.7 0.1 compare_select_fusion.2
  8.8 0.0 copy-start.7
  8.8 0.0 copy-start.8
  8.8 0.0 copy-start.1
  8.9 1.4 gather_fusion.2
  10.2 0.1 rev.6
  10.3 0.7 iota_reduce_fusion.2
  11.6 0.7 iota_reduce_fusion.3
  12.4 0.0 copy-start.5
  12.4 62.6 %all-gather.8.cloned.1.call-done = f32[2,512,512]{2,1,0:T(8,128)} async-done(((f32[2,32,512]{2,1,0:T(8,128)}), f32[2,512,512]{2,1,0:T(8,128)}) %all-gather.8.cloned.1.call-update) | async-done | bytes 2097168 | tf_op jit(solution)/shard_map/all_gather | solution.py:60
  75.0 3.1 fusion.44
  78.1 4.1 %collective-permute-start = (f32[2,64,512]{2,1,0:T(8,128)S(1)}, f32[2,64,512]{2,1,0:T(8,128)S(1)}, u32[]{:S(2)}, u32[]{:S(2)}) collective-permute-start(f32[2,64,512]{2,1,0:T(8,128)S(1)} %fusion.44), channel_id=1, source_target_pairs={{0,16},{16,0},{32,48},{48,32},{64,80},{80,64},{96,112},{112,96},{1... | collective-permute-start | bytes 786440 | tf_op jit(solution)/shard_map/ppermute | solution.py:14
  82.2 0.8 fusion.38
  83.0 0.8 compare_and_fusion
  83.7 0.0 collective-permute-done
  83.8 0.6 gather_fusion.1
  84.4 0.8 broadcast_select_fusion
  85.2 0.0 all-gather.10.cloned.1.call-update
  85.2 0.0 all-gather.6.cloned.1.call-start
  85.2 53.2 %all-gather.12.cloned.1.call-done = f32[1,768,768]{2,1,0:T(8,128)} async-done(((f32[1,48,768]{2,1,0:T(8,128)}), f32[1,768,768]{2,1,0:T(8,128)}) %all-gather.12.cloned.1.call-update) | async-done | bytes 2359312 | tf_op jit(solution)/shard_map/all_gather | solution.py:55
  138.5 0.0 copy-done.6
  138.5 3.9 %fusion.8 = f32[96,768]{1,0:T(8,128)} fusion(f32[1,768,768]{2,1,0:T(8,128)} %all-gather.12.cloned.1.call-done, f32[1,96,768]{2,1,0:T(8,128)S(1)} %copy-done.6), kind=kOutput, calls=%fused_computation.15 | convolution fusion | flops 679477248 | bytes 2949120 | tf_op jit(solution)/shard_map/dot_general | solution.py:18
  142.3 0.0 all-gather.6.cloned.1.call-update
  142.4 0.6 gather_fusion.3
  143.0 1.5 gather_fusion
  144.6 0.1 compare_select_fusion
  144.6 0.0 copy-done.7
  144.6 0.1 multiply_reduce_fusion.1
  144.7 0.0 copy-done.8
  144.7 0.1 and_reduce_fusion
  144.9 0.0 copy-done.1
  144.9 0.6 gather_fusion.4
  145.5 0.1 rev.7
  145.6 0.7 iota_reduce_fusion
  146.9 0.7 iota_reduce_fusion.1
  147.6 0.7 compare_select_fusion.1
  148.3 0.6 gather_fusion.5
  148.9 0.0 copy-done.5
  149.0 0.0 copy-done.4
  149.0 0.7 and_select_fusion
  149.7 59.2 %all-gather.10.cloned.1.call-done = f32[2,1024,512]{2,1,0:T(8,128)} async-done(((f32[2,64,512]{2,1,0:T(8,128)}), f32[2,1024,512]{2,1,0:T(8,128)}) %all-gather.10.cloned.1.call-update) | async-done | bytes 4194320 | tf_op jit(solution)/shard_map/all_gather | solution.py:68
  208.9 13.8 %scatter_custom_fusion = f32[4608,512]{1,0:T(8,128)} fusion(s32[2048]{0:T(1024)S(1)} %bitcast.76, f32[2048,512]{1,0:T(8,128)} %bitcast.77, f32[]{:T(128)} %constant.46.clone.1), kind=kCustom, calls=%fused_computation.7 | custom fusion | bytes 9437696
  222.7 3.7 slice.21
  226.4 1.8 copy-done.2
  228.2 2.1 fusion.22
  230.3 0.0 copy-done.3
  230.3 2.0 fusion.15
  232.3 48.3 %all-gather.6.cloned.1.call-done = f32[1536,768]{1,0:T(8,128)} async-done(((f32[96,768]{1,0:T(8,128)}), f32[1536,768]{1,0:T(8,128)}) %all-gather.6.cloned.1.call-update) | async-done | bytes 4718608 | tf_op jit(solution)/shard_map/all_gather | solution.py:82
  280.7 0.0 copy-done
  280.7 5.3 %fusion.31 = (f32[768]{0:T(1024)S(1)}, f32[768,96]{0,1:T(8,128)S(1)}) fusion(f32[96,768]{1,0:T(8,128)S(1)} %copy-done.3, f32[1536,768]{1,0:T(8,128)} %all-gather.6.cloned.1.call-done, f32[1,96,1536]{2,1,0:T(8,128)S(1)} %copy-done), kind=kOutput, calls=%fused_computation.34 | convolution fusion | flops 1359101184 | bytes 5901312 | tf_op jit(solution)/shard_map/dot_general | solution.py:18
  286.0 3.9 %fusion.2 = f32[2,512,96]{1,2,0:T(8,128)S(1)} fusion(f32[2,2304,512]{2,1,0:T(8,128)} %bitcast.72, f32[768,96]{0,1:T(8,128)S(1)} %get-tuple-element.24), kind=kOutput, calls=%fused_computation.9 | convolution fusion | flops 905969664 | bytes 3833856 | tf_op jit(solution)/shard_map/zt,qtg->qzg/dot_general | solution.py:22
  289.9 6.7 %fusion.21 = f32[2,512]{1,0:T(2,128)S(1)} fusion(f32[2,96,512]{2,1,0:T(8,128)S(1)} %fusion.15, f32[2,512,96]{1,2,0:T(8,128)S(1)} %fusion.2, f32[1,96,1536]{2,1,0:T(8,128)S(1)} %copy-done, f32[2,2304,512]{2,1,0:T(8,128)} %bitcast.73), kind=kOutput, calls=%fused_computation.23 | convolution fusion | flops 1812233216 | bytes 7671808 | tf_op jit(solution)/shard_map/rb,kbm->krm/dot_general | solution.py:22
  296.6 58.2 %all-reduce = (f32[1,768]{1,0:T(1,128)}, f32[2,512]{1,0:T(2,128)S(1)}, f32[2,512]{1,0:T(2,128)S(1)}) all-reduce(f32[1,768]{1,0:T(1,128)S(1)} %broadcast_in_dim.45, f32[2,512]{1,0:T(2,128)S(1)} %multiply_reduce_fusion, f32[2,512]{1,0:T(2,128)S(1)} %add.91), channel_id=1, replica_groups=mesh['leaf'=32,'front'=16] {'front'}, use_global_device_ids=true, to_apply=%region_2.3 | all-reduce | flops 2816 | bytes 22528 | tf_op jit(solution)/shard_map/psum | solution.py:93
  354.8 16.9 %collective-permute-start.1 = (f32[2,512]{1,0:T(2,128)S(1)}, f32[2,512]{1,0:T(2,128)S(1)}, u32[]{:S(2)}, u32[]{:S(2)}) collective-permute-start(f32[2,512]{1,0:T(2,128)S(1)} %get-tuple-element.14), channel_id=1, source_target_pairs={{0,16},{16,0},{32,48},{48,32},{64,80},{80,64},{96,112},{112,96},{1... | collective-permute-start | bytes 12296 | tf_op jit(solution)/shard_map/ppermute | solution.py:14
  371.7 0.2 fusion.36
  371.9 0.6 collective-permute-done.1
  372.5 0.8 fusion.25
  (23 shorter events, 0.2 us)
Async XLA Ops:
  7.2 273.5 %copy-start = (f32[1,96,1536]{2,1,0:T(8,128)S(1)}, f32[1,96,1536]{2,1,0:T(8,128)}, u32[]{:S(2)}) copy-start(f32[1,96,1536]{2,1,0:T(8,128)} %param.11) | copy-start | bytes 1769476
  7.2 131.3 %copy-start.6 = (f32[1,96,768]{2,1,0:T(8,128)S(1)}, f32[1,96,768]{2,1,0:T(8,128)}, u32[]{:S(2)}) copy-start(f32[1,96,768]{2,1,0:T(8,128)} %param.12) | copy-start | bytes 884740
  7.2 67.8 %all-gather.8.cloned.1.call-start = ((), (), s32[]{:S(2)}) async-start(), calls=%async_computation.1 | async-start | bytes 2228224 | tf_op jit(solution)/shard_map/all_gather | solution.py:60
  7.9 130.5 %all-gather.12.cloned.1.call-start = ((), (), s32[]{:S(2)}) async-start(), calls=%async_computation.3 | async-start | bytes 2506752 | tf_op jit(solution)/shard_map/all_gather | solution.py:55
  8.7 200.2 %all-gather.10.cloned.1.call-start = ((), (), s32[]{:S(2)}) async-start(), calls=%async_computation.2 | async-start | bytes 4456448 | tf_op jit(solution)/shard_map/all_gather | solution.py:68
  8.8 135.8 %copy-start.7 = (s32[2]{0:T(128)S(1)}, s32[2]{0:T(128)}, u32[]{:S(2)}) copy-start(s32[2]{0:T(128)} %constant.94) | copy-start | bytes 28
  8.8 135.9 %copy-start.8 = (s32[2]{0:T(128)S(1)}, s32[2]{0:T(128)}, u32[]{:S(2)}) copy-start(s32[2]{0:T(128)} %constant.97) | copy-start | bytes 28
  8.8 136.0 %copy-start.1 = (s32[64]{0:T(128)S(1)}, s32[64]{0:T(128)}, u32[]{:S(2)}) copy-start(s32[64]{0:T(128)} %param.17) | copy-start | bytes 772
  12.4 136.6 %copy-start.5 = (f32[2,32,512]{2,1,0:T(8,128)S(1)}, f32[2,32,512]{2,1,0:T(8,128)}, u32[]{:S(2)}) copy-start(f32[2,32,512]{2,1,0:T(8,128)} %param.15) | copy-start | bytes 393220
  12.4 136.6 %copy-start.4 = (f32[1,48,768]{2,1,0:T(8,128)S(1)}, f32[1,48,768]{2,1,0:T(8,128)}, u32[]{:S(2)}) copy-start(f32[1,48,768]{2,1,0:T(8,128)} %param.13) | copy-start | bytes 442372
  78.1 5.7 %collective-permute-start = (f32[2,64,512]{2,1,0:T(8,128)S(1)}, f32[2,64,512]{2,1,0:T(8,128)S(1)}, u32[]{:S(2)}, u32[]{:S(2)}) collective-permute-start(f32[2,64,512]{2,1,0:T(8,128)S(1)} %fusion.44), channel_id=1, source_target_pairs={{0,16},{16,0},{32,48},{48,32},{64,80},{80,64},{96,112},{112,96},{1... | collective-permute-start | bytes 786440 | tf_op jit(solution)/shard_map/ppermute | solution.py:14
  85.2 195.5 %all-gather.6.cloned.1.call-start = ((), (), s32[]{:S(2)}) async-start(), calls=%async_computation | async-start | bytes 5013504 | tf_op jit(solution)/shard_map/all_gather | solution.py:82
  222.7 5.5 %copy-start.2 = (f32[4608,512]{1,0:T(8,128)S(1)}, f32[4608,512]{1,0:T(8,128)}, u32[]{:S(2)}) copy-start(f32[4608,512]{1,0:T(8,128)} %scatter_custom_fusion) | copy-start | bytes 28311556
  222.7 7.6 %copy-start.3 = (f32[96,768]{1,0:T(8,128)S(1)}, f32[96,768]{1,0:T(8,128)}, u32[]{:S(2)}) copy-start(f32[96,768]{1,0:T(8,128)} %fusion.8) | copy-start | bytes 884740
  354.8 17.7 %collective-permute-start.1 = (f32[2,512]{1,0:T(2,128)S(1)}, f32[2,512]{1,0:T(2,128)S(1)}, u32[]{:S(2)}, u32[]{:S(2)}) collective-permute-start(f32[2,512]{1,0:T(2,128)S(1)} %get-tuple-element.14), channel_id=1, source_target_pairs={{0,16},{16,0},{32,48},{48,32},{64,80},{80,64},{96,112},{112,96},{1... | collective-permute-start | bytes 12296 | tf_op jit(solution)/shard_map/ppermute | solution.py:14
Sparse Core Ops, SparseCore 0:
  11.0 63.9 all-gather.7
  78.0 60.4 all-gather.11
  141.5 67.3 all-gather.9
  211.7 68.8 all-gather.5
where the time goes:
time: 380 us
  waiting for transfers between devices  225 us (59%)
  blocking collectives  58.2 us (15%)
  matrix products  27.9 us (7%)
  local copies, waits for them, and re-layouts  24.9 us (7%)
  starting transfers between devices  21.2 us (6%)
  between operations  15.3 us (4%)
  other arithmetic  6.92 us (2%)
    all_gather x1, waiting for transfers between devices, shards(): lax.all_gather(child_factor_inverse, 'front', axis=1, tiled=True)  62.6 us
    all_gather x1, waiting for transfers between devices, shards(): child_weight = lax.all_gather(selected, 'front', axis=1, tiled=True)  59.2 us
    psum x1, blocking collectives, shards(): lax.psum((parent_block, quad_part, own_part), 'front')  58.2 us
    all_gather x1, waiting for transfers between devices, shards(): lax.all_gather(eliminated_inverse, 'front', axis=0, tiled=True)  53.2 us
    all_gather x1, waiting for transfers between devices, shards(): lax.all_gather(weight_rows, 'front', axis=0, tiled=True)  48.3 us
    ppermute x2, starting transfers between devices, partner_2(): return lax.ppermute(value, axis, pairs)  21 us
    dot_general x5, matrix products, batched_fronts(): jnp.einsum(form, left, right, precision=lax.Precision.HIGHEST, preferred_...  17.8 us
    unnamed x20, local copies, waits for them, and re-layouts  15.7 us
  transfers between devices with their start and end apart: 6, of which 5 were waited for; matrix products, arithmetic and copies ran while one was open for 11% of the time, Pallas kernels for 0%

commit v1 on v0

--- a/solution.py
+++ b/solution.py
@@ -65,7 +65,10 @@
     pooled = jnp.concatenate([own_weights, partner_weights], axis=0)
     slots, kid_ids = children_of(child_parent, leaf_index)
     selected = jnp.take(pooled, slots, axis=0)
-    child_weight = lax.all_gather(selected, "front", axis=1, tiled=True)
+    size = lax.axis_size("front")
+    blocks = jnp.stack([selected for _ in range(size)])
+    blocks = lax.all_to_all(blocks, "front", split_axis=0, concat_axis=0)
+    child_weight = jnp.concatenate(blocks, axis=1)
     index_list = jnp.take(child_index, kid_ids, axis=0)
     placed_rows = (
         jnp.zeros((2, ELIMINATED_SIZE + BORDER_SIZE, CHILD_ELIMINATED), jnp.float32)

time: 380 us -> 349 us (0.918)
  waiting for transfers between devices: 225 us -> 184 us
  local copies, waits for them, and re-layouts: 24.9 us -> 32.2 us
  starting transfers between devices: 21.2 us -> 26.1 us
    all_to_all x0 -> x1, waiting for transfers between devices: none -> 59.6 us  [shards(): blocks = lax.all_to_all(blocks, 'front', split_axis=0, concat_axis=0)]
    all_gather x1 -> x0, waiting for transfers between devices: 59.2 us -> none  [shards(): child_weight = lax.all_gather(selected, 'front', axis=1, tiled=True)]
    all_gather x1, waiting for transfers between devices: 48.3 us -> 0.02 us  [shards(): lax.all_gather(weight_rows, 'front', axis=0, tiled=True)]
    all_gather x1, waiting for transfers between devices: 53.2 us -> 67 us  [shards(): lax.all_gather(eliminated_inverse, 'front', axis=0, tiled=True)]
    all_gather x1, waiting for transfers between devices: 62.6 us -> 55 us  [shards(): lax.all_gather(child_factor_inverse, 'front', axis=1, tiled=True)]
    all_to_all x0 -> x1, starting transfers between devices: none -> 4.86 us  [shards(): blocks = lax.all_to_all(blocks, 'front', split_axis=0, concat_axis=0)]
    all_to_all x0 -> x1, local copies, waits for them, and re-layouts: none -> 4.84 us  [shards(): blocks = lax.all_to_all(blocks, 'front', split_axis=0, concat_axis=0)]
    unnamed x20 -> x18, local copies, waits for them, and re-layouts: 15.7 us -> 15.7 us
  transfers between devices with their start and end apart: 6 -> 6, of which waited for: 5 -> 4; matrix products, arithmetic and copies ran while one was open for 11% -> 14% of each run, Pallas kernels for 0% -> 0%
where the time goes in v1:
time: 349 us; the launch traced here: 348 us
  waiting for transfers between devices  184 us (53%)
  blocking collectives  56.8 us (16%)
  local copies, waits for them, and re-layouts  32.2 us (9%)
  matrix products  28 us (8%)
  starting transfers between devices  26.1 us (7%)
  between operations  15.3 us (4%)
  other arithmetic  6.04 us (2%)
    all_gather x1, waiting for transfers between devices, shards(): lax.all_gather(eliminated_inverse, 'front', axis=0, tiled=True)  67 us
    all_to_all x1, waiting for transfers between devices, shards(): blocks = lax.all_to_all(blocks, 'front', split_axis=0, concat_axis=0)  59.6 us
    psum x1, blocking collectives, shards(): lax.psum((parent_block, quad_part, own_part), 'front')  56.8 us
    all_gather x1, waiting for transfers between devices, shards(): lax.all_gather(child_factor_inverse, 'front', axis=1, tiled=True)  55 us
    ppermute x2, starting transfers between devices, partner_2(): return lax.ppermute(value, axis, pairs)  21.1 us
    dot_general x5, matrix products, batched_fronts(): jnp.einsum(form, left, right, precision=lax.Precision.HIGHEST, preferred_...  17.7 us
    unnamed x18, local copies, waits for them, and re-layouts  15.7 us
    dot_general x4, matrix products, matrix_product(): jnp.dot(left, right, precision=lax.Precision.HIGHEST, preferred_element_t...  10.3 us
  transfers between devices with their start and end apart: 6, of which 4 were waited for; matrix products, arithmetic and copies ran while one was open for 14% of the time, Pallas kernels for 0%

profile of v1, /device:TPU:1, one launch (start us, length us, event | category | flops | bytes accessed | tf_op | source)
XLA Modules:
  0.0 348.2 jit_solution(13975485470752769320)
XLA Ops:
  7.2 0.0 copy-start
  7.2 0.0 all-gather.9.cloned.1.call-start
  7.2 0.7 all-gather.9.cloned.1.call-update
  7.9 0.0 all-gather.7.cloned.1.call-start
  8.0 0.7 all-gather.7.cloned.1.call-update
  8.7 0.0 all-gather.5.cloned.1.call-start
  8.7 67.0 %all-gather.9.cloned.1.call-done = f32[1,768,768]{2,1,0:T(8,128)} async-done(((f32[1,48,768]{2,1,0:T(8,128)}), f32[1,768,768]{2,1,0:T(8,128)}) %all-gather.9.cloned.1.call-update) | async-done | bytes 2359312 | tf_op jit(solution)/shard_map/all_gather | solution.py:55
  75.7 4.0 %fusion.8 = f32[96,768]{1,0:T(8,128)} fusion(f32[1,768,768]{2,1,0:T(8,128)} %all-gather.9.cloned.1.call-done, f32[1,96,768]{2,1,0:T(8,128)} %param.12), kind=kOutput, calls=%fused_computation.15 | convolution fusion | flops 679477248 | bytes 2949120 | tf_op jit(solution)/shard_map/dot_general | solution.py:18
  79.7 0.0 all-gather.5.cloned.1.call-update
  79.7 0.1 compare_select_fusion.2
  79.8 1.3 gather_fusion.2
  81.1 0.1 rev.6
  81.2 0.7 iota_reduce_fusion.2
  82.5 0.7 iota_reduce_fusion.3
  83.2 55.0 %all-gather.7.cloned.1.call-done = f32[2,512,512]{2,1,0:T(8,128)} async-done(((f32[2,32,512]{2,1,0:T(8,128)}), f32[2,512,512]{2,1,0:T(8,128)}) %all-gather.7.cloned.1.call-update) | async-done | bytes 2097168 | tf_op jit(solution)/shard_map/all_gather | solution.py:60
  138.2 3.1 fusion.44
  141.3 4.1 %collective-permute-start = (f32[2,64,512]{2,1,0:T(8,128)S(1)}, f32[2,64,512]{2,1,0:T(8,128)S(1)}, u32[]{:S(2)}, u32[]{:S(2)}) collective-permute-start(f32[2,64,512]{2,1,0:T(8,128)S(1)} %fusion.44), channel_id=1, source_target_pairs={{0,16},{16,0},{32,48},{48,32},{64,80},{80,64},{96,112},{112,96},{1... | collective-permute-start | bytes 786440 | tf_op jit(solution)/shard_map/ppermute | solution.py:14
  145.4 0.7 fusion.38
  146.1 0.7 compare_and_fusion
  146.8 0.0 collective-permute-done
  146.9 0.6 gather_fusion.1
  147.5 0.1 broadcast_select_fusion
  147.6 2.5 stack.80
  150.1 0.0 copy-start.6
  150.1 0.0 copy-start.7
  150.1 0.0 copy-start.1
  150.1 0.0 copy-start.5
  150.1 0.0 copy-start.4
  150.1 4.9 %all-to-all-start = ((f32[16,2,64,512]{3,2,1,0:T(8,128)}), f32[16,2,64,512]{3,2,1,0:T(8,128)}, u32[]{:S(2)}, u32[]{:S(2)}) async-start(f32[16,2,64,512]{3,2,1,0:T(8,128)} %stack.80), calls=%async_computation | async-start | bytes 8388608 | tf_op jit(solution)/shard_map/all_to_all | solution.py:70
  155.0 0.6 gather_fusion.3
  155.6 1.5 gather_fusion
  157.2 0.1 compare_select_fusion
  157.2 0.0 copy-done.6
  157.3 0.1 multiply_reduce_fusion.1
  157.3 0.0 copy-done.7
  157.3 0.1 and_reduce_fusion
  157.5 0.0 copy-done.1
  157.5 0.6 gather_fusion.4
  158.1 0.1 rev.7
  158.2 0.7 iota_reduce_fusion
  159.6 0.7 iota_reduce_fusion.1
  160.2 0.7 compare_select_fusion.1
  160.9 0.6 gather_fusion.5
  161.6 0.0 copy-done.5
  161.6 0.0 copy-done.4
  161.6 0.7 and_select_fusion
  162.3 59.6 %all-to-all-done = f32[16,2,64,512]{3,2,1,0:T(8,128)} async-done(((f32[16,2,64,512]{3,2,1,0:T(8,128)}), f32[16,2,64,512]{3,2,1,0:T(8,128)}, u32[]{:S(2)}, u32[]{:S(2)}) %all-to-all-start) | async-done | bytes 4194336 | tf_op jit(solution)/shard_map/all_to_all | solution.py:70
  222.0 4.8 %copy.9 = f32[16,2,64,512]{3,2,0,1:T(8,128)} copy(f32[16,2,64,512]{3,2,1,0:T(8,128)} %all-to-all-done) | data formatting | bytes 8388608 | tf_op jit(solution)/shard_map/all_to_all | solution.py:70
  226.8 13.8 %scatter_custom_fusion = f32[4608,512]{1,0:T(8,128)} fusion(s32[2048]{0:T(1024)S(1)} %bitcast.79, f32[2048,512]{1,0:T(8,128)} %bitcast.78, f32[]{:T(128)} %constant.46.clone.1), kind=kCustom, calls=%fused_computation.7 | custom fusion | bytes 9437696
  240.6 3.7 %slice.21 = f32[2,1536,512]{2,1,0:T(8,128)S(1)} slice(f32[2,2304,512]{2,1,0:T(8,128)} %bitcast.73), slice={[0:2], [768:2304], [0:512]} | slice | bytes 12582912 | tf_op jit(solution)/shard_map/slice | solution.py:79
  244.3 1.8 copy-done.2
  246.2 2.1 fusion.22
  248.3 0.0 copy-done.3
  248.3 2.0 fusion.15
  250.3 0.0 all-gather.5.cloned.1.call-done
  250.3 0.0 copy-done
  250.3 5.3 %fusion.31 = (f32[768]{0:T(1024)S(1)}, f32[768,96]{0,1:T(8,128)S(1)}) fusion(f32[96,768]{1,0:T(8,128)S(1)} %copy-done.3, f32[1536,768]{1,0:T(8,128)} %all-gather.5.cloned.1.call-done, f32[1,96,1536]{2,1,0:T(8,128)S(1)} %copy-done), kind=kOutput, calls=%fused_computation.34 | convolution fusion | flops 1359101184 | bytes 5901312 | tf_op jit(solution)/shard_map/dot_general | solution.py:18
  255.7 3.9 %fusion.2 = f32[2,512,96]{1,2,0:T(8,128)S(1)} fusion(f32[2,2304,512]{2,1,0:T(8,128)} %bitcast.74, f32[768,96]{0,1:T(8,128)S(1)} %get-tuple-element.24), kind=kOutput, calls=%fused_computation.9 | convolution fusion | flops 905969664 | bytes 3833856 | tf_op jit(solution)/shard_map/zt,qtg->qzg/dot_general | solution.py:22
  259.6 6.7 %fusion.21 = f32[2,512]{1,0:T(2,128)S(1)} fusion(f32[2,96,512]{2,1,0:T(8,128)S(1)} %fusion.15, f32[2,512,96]{1,2,0:T(8,128)S(1)} %fusion.2, f32[1,96,1536]{2,1,0:T(8,128)S(1)} %copy-done, f32[2,2304,512]{2,1,0:T(8,128)} %bitcast.75), kind=kOutput, calls=%fused_computation.23 | convolution fusion | flops 1812233216 | bytes 7671808 | tf_op jit(solution)/shard_map/rb,kbm->krm/dot_general | solution.py:22
  266.3 56.8 %all-reduce = (f32[1,768]{1,0:T(1,128)}, f32[2,512]{1,0:T(2,128)S(1)}, f32[2,512]{1,0:T(2,128)S(1)}) all-reduce(f32[1,768]{1,0:T(1,128)S(1)} %broadcast_in_dim.45, f32[2,512]{1,0:T(2,128)S(1)} %multiply_reduce_fusion, f32[2,512]{1,0:T(2,128)S(1)} %add.91), channel_id=1, replica_groups=mesh['leaf'=32,'front'=16] {'front'}, use_global_device_ids=true, to_apply=%region_2.3 | all-reduce | flops 2816 | bytes 22528 | tf_op jit(solution)/shard_map/psum | solution.py:96
  323.1 17.0 %collective-permute-start.1 = (f32[2,512]{1,0:T(2,128)S(1)}, f32[2,512]{1,0:T(2,128)S(1)}, u32[]{:S(2)}, u32[]{:S(2)}) collective-permute-start(f32[2,512]{1,0:T(2,128)S(1)} %get-tuple-element.14), channel_id=1, source_target_pairs={{0,16},{16,0},{32,48},{48,32},{64,80},{80,64},{96,112},{112,96},{1... | collective-permute-start | bytes 12296 | tf_op jit(solution)/shard_map/ppermute | solution.py:14
  340.1 0.2 fusion.36
  340.3 0.6 collective-permute-done.1
  340.9 0.8 fusion.25
  (22 shorter events, 0.2 us)
Async XLA Ops:
  7.2 243.2 %copy-start = (f32[1,96,1536]{2,1,0:T(8,128)S(1)}, f32[1,96,1536]{2,1,0:T(8,128)}, u32[]{:S(2)}) copy-start(f32[1,96,1536]{2,1,0:T(8,128)} %param.11) | copy-start | bytes 1769476
  7.2 68.5 %all-gather.9.cloned.1.call-start = ((), (), s32[]{:S(2)}) async-start(), calls=%async_computation.3 | async-start | bytes 2506752 | tf_op jit(solution)/shard_map/all_gather | solution.py:55
  7.9 130.3 %all-gather.7.cloned.1.call-start = ((), (), s32[]{:S(2)}) async-start(), calls=%async_computation.2 | async-start | bytes 2228224 | tf_op jit(solution)/shard_map/all_gather | solution.py:60
  8.7 241.7 %all-gather.5.cloned.1.call-start = ((), (), s32[]{:S(2)}) async-start(), calls=%async_computation.1 | async-start | bytes 5013504 | tf_op jit(solution)/shard_map/all_gather | solution.py:85
  141.3 5.5 %collective-permute-start = (f32[2,64,512]{2,1,0:T(8,128)S(1)}, f32[2,64,512]{2,1,0:T(8,128)S(1)}, u32[]{:S(2)}, u32[]{:S(2)}) collective-permute-start(f32[2,64,512]{2,1,0:T(8,128)S(1)} %fusion.44), channel_id=1, source_target_pairs={{0,16},{16,0},{32,48},{48,32},{64,80},{80,64},{96,112},{112,96},{1... | collective-permute-start | bytes 786440 | tf_op jit(solution)/shard_map/ppermute | solution.py:14
  150.1 7.2 %copy-start.6 = (s32[2]{0:T(128)S(1)}, s32[2]{0:T(128)}, u32[]{:S(2)}) copy-start(s32[2]{0:T(128)} %constant.94) | copy-start | bytes 28
  150.1 7.3 %copy-start.7 = (s32[2]{0:T(128)S(1)}, s32[2]{0:T(128)}, u32[]{:S(2)}) copy-start(s32[2]{0:T(128)} %constant.97) | copy-start | bytes 28
  150.1 7.4 %copy-start.1 = (s32[64]{0:T(128)S(1)}, s32[64]{0:T(128)}, u32[]{:S(2)}) copy-start(s32[64]{0:T(128)} %param.17) | copy-start | bytes 772
  150.1 11.5 %copy-start.5 = (f32[2,32,512]{2,1,0:T(8,128)S(1)}, f32[2,32,512]{2,1,0:T(8,128)}, u32[]{:S(2)}) copy-start(f32[2,32,512]{2,1,0:T(8,128)} %param.15) | copy-start | bytes 393220
  150.1 11.5 %copy-start.4 = (f32[1,48,768]{2,1,0:T(8,128)S(1)}, f32[1,48,768]{2,1,0:T(8,128)}, u32[]{:S(2)}) copy-start(f32[1,48,768]{2,1,0:T(8,128)} %param.13) | copy-start | bytes 442372
  150.1 71.9 %all-to-all-start = ((f32[16,2,64,512]{3,2,1,0:T(8,128)}), f32[16,2,64,512]{3,2,1,0:T(8,128)}, u32[]{:S(2)}, u32[]{:S(2)}) async-start(f32[16,2,64,512]{3,2,1,0:T(8,128)} %stack.80), calls=%async_computation | async-start | bytes 8388608 | tf_op jit(solution)/shard_map/all_to_all | solution.py:70
  240.6 5.5 %copy-start.2 = (f32[4608,512]{1,0:T(8,128)S(1)}, f32[4608,512]{1,0:T(8,128)}, u32[]{:S(2)}) copy-start(f32[4608,512]{1,0:T(8,128)} %scatter_custom_fusion) | copy-start | bytes 28311556
  240.6 7.6 %copy-start.3 = (f32[96,768]{1,0:T(8,128)S(1)}, f32[96,768]{1,0:T(8,128)}, u32[]{:S(2)}) copy-start(f32[96,768]{1,0:T(8,128)} %fusion.8) | copy-start | bytes 884740
  323.1 17.8 %collective-permute-start.1 = (f32[2,512]{1,0:T(2,128)S(1)}, f32[2,512]{1,0:T(2,128)S(1)}, u32[]{:S(2)}, u32[]{:S(2)}) collective-permute-start(f32[2,512]{1,0:T(2,128)S(1)} %get-tuple-element.14), channel_id=1, source_target_pairs={{0,16},{16,0},{32,48},{48,32},{64,80},{80,64},{96,112},{112,96},{1... | collective-permute-start | bytes 12296 | tf_op jit(solution)/shard_map/ppermute | solution.py:14
Sparse Core Ops, SparseCore 0:
  11.0 64.6 all-gather.8
  78.7 59.4 all-gather.6
  141.2 105.2 all-gather.4
